TPU v7x, 32 devices: a whole 2x2x4 slice. The times are simulated.
32 devices in a mesh: groups: 1, fac: 32 (over z, y, x, core).
Axes of the slice: x: 2, y: 2, z: 4, core: 2. Of those that a mesh axis runs over, the one named last changes fastest.
Arguments:
- sky_image: float32 [64, 96, 4096], P(('groups', 'fac')), may hold values from 0 to 18, as said below
- measured_real: float32 [64, 96, 4096], P(('groups', 'fac')), may hold values from -6 to 6
- measured_imaginary: float32 [64, 96, 4096], P(('groups', 'fac')), may hold values from -6 to 6
- sampling_mask: int32 [64, 96, 4096], P(('groups', 'fac')), may hold values 0 or 1
- dual_field: float32 [64, 96, 4096], P('groups', None, 'fac'), may hold values from -6 to 6
Outputs:
- next_image: float32 [64, 96, 4096], P(('groups', 'fac'))
- next_dual: float32 [64, 96, 4096], P('groups', None, 'fac')
Inputs may be any that keep to these rules, and one draw needn't show every extreme that they name: `sky_image`: non-negative sky brightness.
All inputs are finite; a program needn't handle non-finite values. No bound on the sum of `sampling_mask` on one device may be relied on, other than what follows from the above.
Results may differ from a plain program's by a relative error of at most 0.00012.
Values sent between devices are 32-bit elements; how exact they have to be, the bound alone decides.
No kernel may reach another device: no remote copies, remote signals or barrier semaphores. Data moves between devices by JAX's collectives and lax.ppermute only.
A program may use at most 192 MiB of HBM per device.

v0:
```python
import jax
import jax.numpy as jnp
import numpy as np
from jax import lax
from jax.sharding import PartitionSpec as P

LEVELS = 4
low_pass = (
    0.2303778133088964,
    0.7148465705529155,
    0.6308807679298587,
    -0.0279837694168599,
    -0.1870348117190931,
    0.0308413818355607,
    0.0328830116668852,
    -0.010597401785069,
)
high_pass = tuple(((-1) ** tap_index * low_pass[7 - tap_index] for tap_index in range(8)))
primal_step = 0.6
dual_step = 0.8
ball_radius = 12.0
precise = lax.Precision.HIGHEST


def contract(pattern, left_side, right_side):
    return jnp.einsum(
        pattern, left_side, right_side, precision=precise, preferred_element_type=jnp.float32
    )


def fourier_table(length, direction):
    sample_grid = np.arange(length)
    angles = 2.0 * np.pi * (np.outer(sample_grid, sample_grid) % length) / length
    factor = 1.0 / np.sqrt(length)
    return (
        jnp.asarray(np.cos(angles) * factor, jnp.float32),
        jnp.asarray(direction * np.sin(angles) * factor, jnp.float32),
    )


def twist_table(inner_size, outer_size, length, direction):
    angles = (
        2.0
        * np.pi
        * (np.arange(inner_size)[:, None] * np.arange(outer_size)[None, :] % length)
        / length
    )
    return (
        jnp.asarray(np.cos(angles), jnp.float32),
        jnp.asarray(direction * np.sin(angles), jnp.float32),
    )


def complex_step(real_part, imag_part, pattern, matrix):
    if imag_part is None:
        return (contract(pattern, real_part, matrix[0]), contract(pattern, real_part, matrix[1]))
    return (
        contract(pattern, real_part, matrix[0]) - contract(pattern, imag_part, matrix[1]),
        contract(pattern, real_part, matrix[1]) + contract(pattern, imag_part, matrix[0]),
    )


def data_gradient(sky_image, measured_real, measured_imaginary, sampling_mask):
    channels, row_count, column_count = sky_image.shape
    outer_size = 64
    inner_size = column_count // outer_size
    sample_grid = sky_image.reshape(channels, row_count, inner_size, outer_size)
    real_part, imag_part = complex_step(
        sample_grid, None, "crba,rs->csba", fourier_table(row_count, -1.0)
    )
    real_part, imag_part = complex_step(
        real_part, imag_part, "csba,bk->cska", fourier_table(inner_size, -1.0)
    )
    twist_real, twist_imag = twist_table(inner_size, outer_size, column_count, -1.0)
    real_part, imag_part = (
        real_part * twist_real - imag_part * twist_imag,
        real_part * twist_imag + imag_part * twist_real,
    )
    real_part, imag_part = complex_step(
        real_part, imag_part, "cska,aj->csjk", fourier_table(outer_size, -1.0)
    )
    weights = sampling_mask.astype(jnp.float32)
    real_part = weights * (real_part.reshape(channels, row_count, column_count) - measured_real)
    imag_part = weights * (
        imag_part.reshape(channels, row_count, column_count) - measured_imaginary
    )
    real_part = real_part.reshape(channels, row_count, outer_size, inner_size)
    imag_part = imag_part.reshape(channels, row_count, outer_size, inner_size)
    real_part, imag_part = complex_step(
        real_part, imag_part, "csjk,ja->cska", fourier_table(outer_size, 1.0)
    )
    twist_real, twist_imag = twist_table(inner_size, outer_size, column_count, 1.0)
    real_part, imag_part = (
        real_part * twist_real - imag_part * twist_imag,
        real_part * twist_imag + imag_part * twist_real,
    )
    real_part, imag_part = complex_step(
        real_part, imag_part, "cska,kb->csba", fourier_table(inner_size, 1.0)
    )
    row_real, row_imag = fourier_table(row_count, 1.0)
    result = contract("csba,sr->crba", real_part, row_real) - contract(
        "csba,sr->crba", imag_part, row_imag
    )
    return result.reshape(channels, row_count, column_count)


def row_matrix(length):
    current = np.eye(length)
    details = []
    for level_index in range(LEVELS):
        width_now = current.shape[0]
        half_size = width_now // 2
        lower = np.zeros((half_size, width_now))
        upper = np.zeros((half_size, width_now))
        for target in range(half_size):
            for tap_index in range(8):
                lower[target, (2 * target + tap_index) % width_now] += low_pass[tap_index]
                upper[target, (2 * target + tap_index) % width_now] += high_pass[tap_index]
        details.insert(0, upper @ current)
        current = lower @ current
    return jnp.asarray(np.concatenate([current] + details, 0), jnp.float32)


def analysis_step(length):
    half_size = length // 2
    matrix = np.zeros((length + 6, length))
    for target in range(half_size):
        for tap_index in range(8):
            matrix[2 * target + tap_index, target] += low_pass[tap_index]
            matrix[2 * target + tap_index, half_size + target] += high_pass[tap_index]
    return jnp.asarray(matrix, jnp.float32)


def synthesis_step(length):
    matrix = np.zeros((2 * (length + 3), 2 * length))
    for source in range(length):
        for parity in range(2):
            for back_step in range(4):
                matrix[source - back_step + 3, 2 * source + parity] += low_pass[
                    parity + 2 * back_step
                ]
                matrix[length + 3 + source - back_step + 3, 2 * source + parity] += high_pass[
                    parity + 2 * back_step
                ]
    return jnp.asarray(matrix, jnp.float32)


def column_analysis(values, right_rim):
    coarse = values
    details = []
    for level_index in range(LEVELS):
        length = coarse.shape[-1]
        extended = jnp.concatenate([coarse, right_rim(coarse[..., :6])], -1)
        halves = contract("...m,mk->...k", extended, analysis_step(length))
        details.insert(0, halves[..., length // 2 :])
        coarse = halves[..., : length // 2]
    return jnp.concatenate([coarse] + details, -1)


def column_synthesis(coefficients, left_rim):
    length = coefficients.shape[-1] >> LEVELS
    coarse = coefficients[..., :length]
    offset = length
    for level_index in range(LEVELS):
        detail = coefficients[..., offset : offset + length]
        coarse_edge, detail_edge = left_rim(coarse[..., -3:], detail[..., -3:])
        extended = jnp.concatenate([coarse_edge, coarse, detail_edge, detail], -1)
        coarse = contract("...m,mk->...k", extended, synthesis_step(length))
        offset = offset + length
        length = length * 2
    return coarse


def right_within(edge_cols):
    return jnp.roll(edge_cols, -1, axis=-2)


def left_within(coarse_edge, detail_edge):
    return (jnp.roll(coarse_edge, 1, axis=-2), jnp.roll(detail_edge, 1, axis=-2))


def shards(sky_image, measured_real, measured_imaginary, sampling_mask, dual_field):
    channels, row_count, column_count = sky_image.shape
    rows_table = row_matrix(row_count)
    gradient = data_gradient(sky_image, measured_real, measured_imaginary, sampling_mask)
    facet_count = lax.axis_size("fac")
    facet_width = column_count // facet_count
    local_dual = lax.all_to_all(dual_field, "fac", split_axis=0, concat_axis=2, tiled=True)
    coefficients = local_dual.reshape(channels, row_count, facet_count, facet_width)
    prior_term = column_synthesis(coefficients, left_within).reshape(
        channels, row_count, column_count
    )
    prior_term = contract("sr,csn->crn", rows_table, prior_term)
    next_image = jnp.maximum(sky_image - primal_step * (gradient + prior_term), 0.0)
    analysed = contract("rs,csn->crn", rows_table, 2.0 * next_image - sky_image)
    analysed = column_analysis(
        analysed.reshape(channels, row_count, facet_count, facet_width), right_within
    )
    lifted = local_dual + dual_step * analysed.reshape(channels, row_count, column_count)
    summed = lax.psum(jnp.sum(lifted * lifted, axis=0), "fac")
    shrunk = lifted / jnp.maximum(1.0, jnp.sqrt(summed) / ball_radius)
    next_dual = lax.all_to_all(shrunk, "fac", split_axis=2, concat_axis=0, tiled=True)
    return (next_image, next_dual)


def solution(mesh):
    return jax.shard_map(
        shards,
        mesh=mesh,
        in_specs=(
            P(("groups", "fac"), None, None),
            P(("groups", "fac"), None, None),
            P(("groups", "fac"), None, None),
            P(("groups", "fac"), None, None),
            P("groups", None, "fac"),
        ),
        out_specs=(P(("groups", "fac"), None, None), P("groups", None, "fac")),
        check_vma=False,
    )
```

profile of v0, /device:TPU:0, one launch (start us, length us, event | category | flops | bytes accessed | tf_op | source)
XLA Modules:
  0.0 563.5 jit_solution(9362236796377634353)
XLA Ops:
  7.2 7.4 %all-to-all-start = ((f32[64,96,128]{2,1,0:T(8,128)}), f32[64,96,128]{2,1,0:T(8,128)}, u32[]{:S(2)}, u32[]{:S(2)}) async-start(f32[64,96,128]{2,1,0:T(8,128)} %param.34), calls=%async_computation | async-start | bytes 6291456 | tf_op jit(solution)/shard_map/all_to_all | solution.py:188
  34.0 6.8 %fusion.35 = f32[2,96,64,64]{1,3,2,0:T(8,128)S(1)} fusion(f32[64,64,1,1]{0,1,3,2:T(8,128)S(1)} %copy-done.10, f32[2,96,64,64]{1,3,2,0:T(8,128)S(1)} %bitcast.155), kind=kOutput, calls=%fused_computation.54 | convolution fusion | flops 603979776 | bytes 6307840 | tf_op jit(solution)/shard_map/csba,bk->cska/dot_general | solution.py:26
  40.8 6.6 %fusion.60 = f32[2,96,64,64]{1,3,2,0:T(8,128)S(1)} fusion(f32[2,96,64,64]{1,3,2,0:T(8,128)S(1)} %fusion.37, f32[64,64,1,1]{0,1,3,2:T(8,128)S(1)} %copy-done.10, f32[2,96,64,64]{1,3,2,0:T(8,128)S(1)} %bitcast.152), kind=kOutput, calls=%fused_computation.80 | convolution fusion | flops 604766208 | bytes 9453568 | tf_op jit(solution)/shard_map/csba,bk->cska/dot_general | solution.py:26
  47.5 11.3 %fusion.13 = (f32[2,96,64,64]{1,2,3,0:T(8,128)}, f32[2,96,64,64]{1,2,3,0:T(8,128)S(1)}) fusion(f32[2,96,64,64]{1,3,2,0:T(8,128)S(1)} %fusion.60, f32[64,64]{0,1:T(8,128)S(1)} %copy-done.15, f32[64,64]{0,1:T(8,128)S(1)} %copy-done.9, f32[2,96,64,64]{1,3,2,0:T(8,128)S(1)} %fusion.35, f32[64,64,1,1]{0,1,3,2:T(8,128)S(1)} %copy-done.13, ...), kind=kOutput, calls=%fused_computation.20 | convolution fusion | flops 609484800 | bytes 15777792 | tf_op jit(solution)/shard_map/csba,bk->cska/dot_general | solution.py:26
  58.7 7.1 %fusion.29 = f32[2,96,64,64]{1,3,2,0:T(8,128)} fusion(f32[64,64,1,1]{0,1,3,2:T(8,128)S(1)} %copy-done.13, f32[2,96,64,64]{1,2,3,0:T(8,128)S(1)} %get-tuple-element.5), kind=kOutput, calls=%fused_computation.48 | convolution fusion | flops 603979776 | bytes 6307840 | tf_op jit(solution)/shard_map/cska,aj->csjk/dot_general | solution.py:26
  65.8 7.1 %fusion.27 = f32[2,96,64,64]{1,3,2,0:T(8,128)} fusion(f32[64,64,1,1]{0,1,3,2:T(8,128)S(1)} %copy-done.10, f32[2,96,64,64]{1,2,3,0:T(8,128)S(1)} %get-tuple-element.5), kind=kOutput, calls=%fused_computation.46 | convolution fusion | flops 603979776 | bytes 6307840 | tf_op jit(solution)/shard_map/cska,aj->csjk/dot_general | solution.py:26
  78.2 9.7 %subtract_bitcast_fusion.1 = f32[2,96,64,64]{1,2,3,0:T(8,128)S(1)} fusion(f32[2,96,64,64]{1,3,2,0:T(8,128)} %fusion.29, f32[64,64,1,1]{0,1,3,2:T(8,128)S(1)} %copy-done.10, f32[2,96,64,64]{1,2,3,0:T(8,128)} %get-tuple-element.4), kind=kOutput, calls=%fused_computation.37 | convolution fusion | flops 604766208 | bytes 9453568 | tf_op jit(solution)/shard_map/cska,aj->csjk/dot_general | solution.py:26
  102.7 9.7 %add_bitcast_fusion.1 = f32[2,96,64,64]{1,2,3,0:T(8,128)S(1)} fusion(f32[2,96,64,64]{1,3,2,0:T(8,128)} %fusion.27, f32[64,64,1,1]{0,1,3,2:T(8,128)S(1)} %copy-done.13, f32[2,96,64,64]{1,2,3,0:T(8,128)} %get-tuple-element.4), kind=kOutput, calls=%fused_computation.36 | convolution fusion | flops 604766208 | bytes 9453568 | tf_op jit(solution)/shard_map/cska,aj->csjk/dot_general | solution.py:26
  116.7 11.3 %fusion.12 = (f32[2,96,4096]{1,2,0:T(8,128)}, f32[2,96,4096]{1,2,0:T(8,128)}) fusion(f32[2,96,4096]{1,2,0:T(8,128)} %copy.132, f32[2,96,64,64]{1,3,2,0:T(8,128)} %copy.131, s32[2,96,4096]{1,2,0:T(8,128)} %copy.123, f32[2,96,4096]{1,2,0:T(8,128)} %copy.137, f32[2,96,64,64]{1,3,2,0:T(8,128)} %copy.136), kind=kLoop, calls=%fused_computation.17 | loop fusion | flops 3932160 | bytes 22020096 | tf_op jit(solution)/shard_map/mul | solution.py:83
  128.0 10.9 %fusion.19 = f32[2,96,64,64]{1,3,2,0:T(8,128)} fusion(f32[64,64,1,1]{0,1,3,2:T(8,128)S(1)} %copy-done.10, f32[2,96,64,64]{1,3,2,0:T(8,128)} %bitcast.164), kind=kOutput, calls=%fused_computation.38 | convolution fusion | flops 603979776 | bytes 6307840 | tf_op jit(solution)/shard_map/csjk,ja->cska/dot_general | solution.py:26
  138.9 7.1 %fusion.21 = f32[2,96,64,64]{1,3,2,0:T(8,128)} fusion(f32[64,64,1,1]{0,1,3,2:T(8,128)S(1)} %copy-done.12, f32[2,96,64,64]{1,3,2,0:T(8,128)S(1)} %bitcast.165), kind=kOutput, calls=%fused_computation.40 | convolution fusion | flops 603979776 | bytes 6307840 | tf_op jit(solution)/shard_map/csjk,ja->cska/dot_general | solution.py:26
  146.0 7.1 %fusion.23 = f32[2,96,64,64]{1,3,2,0:T(8,128)} fusion(f32[64,64,1,1]{0,1,3,2:T(8,128)S(1)} %copy-done.12, f32[2,96,64,64]{1,3,2,0:T(8,128)S(1)} %bitcast.162), kind=kOutput, calls=%fused_computation.42 | convolution fusion | flops 603979776 | bytes 6307840 | tf_op jit(solution)/shard_map/csjk,ja->cska/dot_general | solution.py:26
  153.1 7.2 %fusion.25 = f32[2,96,64,64]{1,3,2,0:T(8,128)} fusion(f32[64,64,1,1]{0,1,3,2:T(8,128)S(1)} %copy-done.10, f32[2,96,64,64]{1,3,2,0:T(8,128)S(1)} %bitcast.163), kind=kOutput, calls=%fused_computation.44 | convolution fusion | flops 603979776 | bytes 6307840 | tf_op jit(solution)/shard_map/csjk,ja->cska/dot_general | solution.py:26
  160.3 17.0 %copy_add_fusion = (f32[2,96,64,64]{1,2,3,0:T(8,128)S(1)}, f32[2,96,64,64]{1,2,3,0:T(8,128)}) fusion(f32[2,96,64,64]{1,3,2,0:T(8,128)} %fusion.19, f32[2,96,64,64]{1,3,2,0:T(8,128)} %fusion.23, f32[2,96,64,64]{1,3,2,0:T(8,128)} %fusion.21, f32[2,96,64,64]{1,3,2,0:T(8,128)} %fusion.25), kind=kLoop, calls=%fused_computation.29 | loop fusion | flops 1572864 | bytes 18874368 | tf_op jit(solution)/shard_map/add | solution.py:59
  177.3 6.7 %fusion.74 = f32[2,96,64,64]{1,3,2,0:T(8,128)S(1)} fusion(f32[64,64,1,1]{0,1,3,2:T(8,128)S(1)} %copy-done.12, f32[2,96,64,64]{1,2,3,0:T(8,128)S(1)} %get-tuple-element.26, f32[2,96,64,64]{1,2,3,0:T(8,128)} %get-tuple-element.27, f32[64,64]{0,1:T(8,128)S(1)} %copy-done.11, f32[64,64]{0,1:T(8,128)S(1)} %copy-done.9), kind=kOutput, calls=%fused_computation.85 | convolution fusion | flops 606339072 | bytes 9486336 | tf_op jit(solution)/shard_map/cska,kb->csba/dot_general | solution.py:26
  206.8 7.4 %fusion.70 = f32[2,64,64,96]{3,2,1,0:T(8,128)} fusion(f32[2,64,64,96]{3,2,1,0:T(8,128)S(1)} %fusion.15, f32[96,96,1,1]{1,0,3,2:T(8,128)S(1)} %copy-done.18, f32[2,96,64,64]{1,2,3,0:T(8,128)S(1)} %subtract_bitcast_fusion), kind=kOutput, calls=%fused_computation.82 | convolution fusion | flops 906756096 | bytes 9474048 | tf_op jit(solution)/shard_map/csba,sr->crba/dot_general | solution.py:26
  235.5 7.8 %copy.148 = f32[2,96,32,134]{3,2,1,0:T(8,128)} copy(f32[2,96,32,134]{1,3,2,0:T(8,128)} %pad_maximum_fusion) | data formatting | bytes 6586368 | tf_op jit(solution)/shard_map/concatenate | solution.py:167
  243.3 8.3 %fusion.128 = f32[2,96,32,128]{3,2,1,0:T(8,128)} fusion(f32[2,96,32,134]{3,2,1,0:T(8,128)} %copy.148, f32[134,128,1,1]{1,0,3,2:T(8,128)S(1)} %copy-done.17), kind=kOutput, calls=%fused_computation.138 | convolution fusion | flops 1264582656 | bytes 6507520 | tf_op jit(solution)/shard_map/...m,mk->...k/dot_general | solution.py:26
  276.0 8.4 %fusion.43 = f32[2,96,32,64]{1,3,2,0:T(8,128)S(1)} fusion(f32[70,64,1,1]{0,1,3,2:T(8,128)S(1)} %copy-done.22, f32[2,96,32,70]{3,2,1,0:T(8,128)S(1)} %maximum_maximum_fusion), kind=kOutput, calls=%fused_computation.63 | convolution fusion | flops 330301440 | bytes 3311104 | tf_op jit(solution)/shard_map/...m,mk->...k/dot_general | solution.py:26
  292.7 7.0 %multiply_reduce_fusion = (f32[96,32,128]{0,2,1:T(8,128)}, f32[2,96,32,128]{1,3,2,0:T(8,128)}) fusion(f32[2,96,32,64]{1,3,2,0:T(8,128)} %copy.170, f32[2,96,32,32]{1,3,2,0:T(8,128)} %get-tuple-element.23, f32[2,96,32,16]{1,3,2,0:T(8,128)} %get-tuple-element.25, f32[2,96,32,16]{1,3,2,0:T(8,128)S(1)} %fusion.106, f32[32,2,96,128]{2,3,0,1:T(8,128)} %copy.147), kind=kLoop, calls=%fused_computation.31 | loop fusion | flops 5111808 | bytes 11010048 | tf_op jit(solution)/shard_map/reduce_sum | solution.py:200
  299.6 135.1 %all-reduce.2.cloned.1.call-done = f32[96,4096]{0,1:T(8,128)} async-done(((f32[96,4096]{0,1:T(8,128)}), f32[96,4096]{0,1:T(8,128)}) %all-reduce.2.cloned.1.call-update) | async-done | bytes 1572880 | tf_op jit(solution)/shard_map/psum | solution.py:200
  437.6 15.1 %copy_divide_fusion = f32[2,96,4096]{1,0,2:T(2,128)S(1)} fusion(f32[2,96,4096]{1,2,0:T(8,128)S(1)} %bitcast.169, f32[96,4096]{0,1:T(8,128)S(1)} %multiply_maximum_fusion), kind=kLoop, calls=%fused_computation.24 | loop fusion | flops 786432 | bytes 7864320 | tf_op jit(solution)/shard_map/div | solution.py:201
  452.7 97.1 %all_to_all.33 = f32[2,96,4096]{1,0,2:T(2,128)} all-to-all(f32[2,96,4096]{1,0,2:T(2,128)S(1)} %copy_divide_fusion), channel_id=1, replica_groups=mesh['groups'=1,'fac'=32] {'fac'}, dimensions={2} | all-to-all | bytes 6291456 | tf_op jit(solution)/shard_map/all_to_all | solution.py:202
  549.8 6.6 %copy.154 = f32[32,2,96,128]{3,2,1,0:T(8,128)} copy(f32[32,2,96,128]{2,1,3,0:T(2,128)} %bitcast.171) | data formatting | bytes 6291456 | tf_op jit(solution)/shard_map/all_to_all | solution.py:202
  (111 shorter events, 123.0 us)
Async XLA Ops:
  7.2 7.5 %copy-start.5 = (f32[2,96,4096]{2,1,0:T(8,128)S(1)}, f32[2,96,4096]{2,1,0:T(8,128)}, u32[]{:S(2)}) copy-start(f32[2,96,4096]{2,1,0:T(8,128)} %param.30) | copy-start | bytes 9437188
  7.2 212.3 %all-to-all-start = ((f32[64,96,128]{2,1,0:T(8,128)}), f32[64,96,128]{2,1,0:T(8,128)}, u32[]{:S(2)}, u32[]{:S(2)}) async-start(f32[64,96,128]{2,1,0:T(8,128)} %param.34), calls=%async_computation | async-start | bytes 6291456 | tf_op jit(solution)/shard_map/all_to_all | solution.py:188
  14.6 3.4 copy-start.20
  14.6 420.1 %all-reduce.2.cloned.1.call-start = ((), (), s32[]{:S(2)}) async-start(), calls=%async_computation.2 | async-start | bytes 4194304 | tf_op jit(solution)/shard_map/psum | solution.py:200
  18.0 5.8 %copy-start.1 = (f32[2,96,4096]{1,2,0:T(8,128)S(1)}, f32[2,96,4096]{1,2,0:T(8,128)}, u32[]{:S(2)}) copy-start(f32[2,96,4096]{1,2,0:T(8,128)} %copy.124) | copy-start | bytes 9437188
  18.0 5.8 %copy-start.21 = (f32[96,96]{1,0:T(8,128)S(1)}, f32[96,96]{1,0:T(8,128)}, u32[]{:S(2)}) copy-start(f32[96,96]{1,0:T(8,128)} %constant.51.clone) | copy-start | bytes 110596
  23.8 3.6 copy-start.13
  27.4 6.6 %copy-start.10 = (f32[64,64,1,1]{0,1,3,2:T(8,128)S(1)}, f32[64,64,1,1]{0,1,3,2:T(8,128)}, u32[]{:S(2)}) copy-start(f32[64,64,1,1]{0,1,3,2:T(8,128)} %constant.72) | copy-start | bytes 49156
  40.8 6.6 %copy-start.9 = (f32[64,64]{0,1:T(8,128)S(1)}, f32[64,64]{0,1:T(8,128)}, u32[]{:S(2)}) copy-start(f32[64,64]{0,1:T(8,128)} %constant.55.clone) | copy-start | bytes 49156
  40.8 6.6 %copy-start.15 = (f32[64,64]{0,1:T(8,128)S(1)}, f32[64,64]{0,1:T(8,128)}, u32[]{:S(2)}) copy-start(f32[64,64]{0,1:T(8,128)} %constant.56.clone) | copy-start | bytes 49156
  128.0 10.9 %copy-start.4 = (f32[2,96,4096]{1,2,0:T(8,128)S(1)}, f32[2,96,4096]{1,2,0:T(8,128)}, u32[]{:S(2)}) copy-start(f32[2,96,4096]{1,2,0:T(8,128)} %get-tuple-element.19) | copy-start | bytes 9437188
  128.0 10.9 %copy-start.12 = (f32[64,64,1,1]{0,1,3,2:T(8,128)S(1)}, f32[64,64,1,1]{0,1,3,2:T(8,128)}, u32[]{:S(2)}) copy-start(f32[64,64,1,1]{0,1,3,2:T(8,128)} %constant.74) | copy-start | bytes 49156
  138.9 7.1 %copy-start.3 = (f32[2,96,4096]{1,2,0:T(8,128)S(1)}, f32[2,96,4096]{1,2,0:T(8,128)}, u32[]{:S(2)}) copy-start(f32[2,96,4096]{1,2,0:T(8,128)} %get-tuple-element.18) | copy-start | bytes 9437188
  160.3 17.0 %copy-start.11 = (f32[64,64]{0,1:T(8,128)S(1)}, f32[64,64]{0,1:T(8,128)}, u32[]{:S(2)}) copy-start(f32[64,64]{0,1:T(8,128)} %constant.58.clone) | copy-start | bytes 49156
  177.3 6.7 %copy-start = (f32[2,96,64,64]{1,2,3,0:T(8,128)S(1)}, f32[2,96,64,64]{1,2,3,0:T(8,128)}, u32[]{:S(2)}) copy-start(f32[2,96,64,64]{1,2,3,0:T(8,128)} %get-tuple-element.27) | copy-start | bytes 9437188
  184.0 5.6 copy-start.19
  201.5 5.4 copy-start.18
  224.7 3.2 copy-start.27
  235.5 7.8 %copy-start.17 = (f32[134,128,1,1]{1,0,3,2:T(8,128)S(1)}, f32[134,128,1,1]{1,0,3,2:T(8,128)}, u32[]{:S(2)}) copy-start(f32[134,128,1,1]{1,0,3,2:T(8,128)} %constant.80) | copy-start | bytes 205828
  251.6 4.9 copy-start.6
  251.6 5.0 copy-start.14
  262.8 3.4 copy-start.8
  276.0 9.6 %copy-start.23 = (f32[38,32,1,1]{0,1,3,2:T(8,128)S(1)}, f32[38,32,1,1]{0,1,3,2:T(8,128)}, u32[]{:S(2)}) copy-start(f32[38,32,1,1]{0,1,3,2:T(8,128)} %constant.84) | copy-start | bytes 14596
  286.7 4.2 copy-start.24
  (6 other events, 11.5 us)
Sparse Core Ops, SparseCore 0:
  299.8 134.9 all-reduce.1
where the time goes:
time: 567 us; the launch traced here: 563 us
  matrix products  183 us (32%)
  waiting for transfers between devices  135 us (24%)
  blocking collectives  97.1 us (17%)
  local copies, waits for them, and re-layouts  69.9 us (12%)
  other arithmetic  56.4 us (10%)
  between operations  14.9 us (3%)
  starting transfers between devices  7.46 us (1%)
    dot_general x28, matrix products, contract(): jnp.einsum(pattern, left_side, right_side, precision=precise, preferred_e...  173 us
    psum x1, waiting for transfers between devices, shards(): summed = lax.psum(jnp.sum(lifted * lifted, axis=0), 'fac')  135 us
    all_to_all x1, blocking collectives, shards(): lax.all_to_all(shrunk, 'fac', split_axis=2, concat_axis=0, tiled=True)  97.1 us
    unnamed x62, local copies, waits for them, and re-layouts  24.6 us
    add x1, other arithmetic, complex_step(): contract(pattern, real_part, matrix[1])  17 us
    div x1, other arithmetic, shards(): shrunk = lifted / jnp.maximum(1.0, jnp.sqrt(summed) / ball_radius)  15.1 us
  transfers between devices with their start and end apart: 2, of which 1 were waited for; matrix products, arithmetic and copies ran while one was open for 36% of the time, Pallas kernels for 0%

commit v1 on v0

--- a/solution.py
+++ b/solution.py
@@ -180,12 +180,20 @@
 
 
 def shards(sky_image, measured_real, measured_imaginary, sampling_mask, dual_field):
+
+    def review_wires(view):
+        local_next = jnp.split(view, jax.lax.psum(1, axis_name="fac"), 0)
+        answer = jnp.stack(local_next, axis=0)
+        v_next = jax.lax.all_to_all(answer, axis_name="fac", split_axis=0, concat_axis=0)
+        reached = jnp.concatenate(v_next, axis=2)
+        return reached
+
     channels, row_count, column_count = sky_image.shape
     rows_table = row_matrix(row_count)
     gradient = data_gradient(sky_image, measured_real, measured_imaginary, sampling_mask)
     facet_count = lax.axis_size("fac")
     facet_width = column_count // facet_count
-    local_dual = lax.all_to_all(dual_field, "fac", split_axis=0, concat_axis=2, tiled=True)
+    local_dual = review_wires(dual_field)
     coefficients = local_dual.reshape(channels, row_count, facet_count, facet_width)
     prior_term = column_synthesis(coefficients, left_within).reshape(
         channels, row_count, column_count

time: 567 us -> 618 us (1.090)
  local copies, waits for them, and re-layouts: 69.9 us -> 119 us
    unnamed x62 -> x93, local copies, waits for them, and re-layouts: 24.6 us -> 72.4 us
  transfers between devices with their start and end apart: 2 -> 2, of which waited for: 1 -> 1; matrix products, arithmetic and copies ran while one was open for 36% -> 33% of each run, Pallas kernels for 0% -> 0%
where the time goes in v1:
time: 618 us; the launch traced here: 613 us
  matrix products  183 us (30%)
  waiting for transfers between devices  135 us (22%)
  local copies, waits for them, and re-layouts  119 us (19%)
  blocking collectives  97.1 us (16%)
  other arithmetic  56.4 us (9%)
  between operations  14.9 us (2%)
  starting transfers between devices  7.45 us (1%)
    dot_general x28, matrix products, contract(): jnp.einsum(pattern, left_side, right_side, precision=precise, preferred_e...  173 us
    psum x1, waiting for transfers between devices, shards(): summed = lax.psum(jnp.sum(lifted * lifted, axis=0), 'fac')  135 us
    all_to_all x1, blocking collectives, shards(): lax.all_to_all(shrunk, 'fac', split_axis=2, concat_axis=0, tiled=True)  97.1 us
    unnamed x93, local copies, waits for them, and re-layouts  72.4 us
    add x1, other arithmetic, complex_step(): contract(pattern, real_part, matrix[1])  17 us
    div x1, other arithmetic, shards(): shrunk = lifted / jnp.maximum(1.0, jnp.sqrt(summed) / ball_radius)  15.1 us
  transfers between devices with their start and end apart: 2, of which 1 were waited for; matrix products, arithmetic and copies ran while one was open for 33% of the time, Pallas kernels for 0%

profile of v1, /device:TPU:0, one launch (start us, length us, event | category | flops | bytes accessed | tf_op | source)
XLA Modules:
  0.0 612.9 jit_solution(10371218485542925350)
XLA Ops:
  56.6 7.4 %all-to-all-start = ((f32[32,2,96,128]{3,2,1,0:T(8,128)}), f32[32,2,96,128]{3,2,1,0:T(8,128)}, u32[]{:S(2)}, u32[]{:S(2)}) async-start(f32[32,2,96,128]{3,2,1,0:T(8,128)} %bitcast_dynamic-update-slice_fusion), calls=%async_computation | async-start | bytes 6291456 | tf_op jit(solution)/shard_map/all_to_all | solution.py:187
  83.4 6.8 %fusion.35 = f32[2,96,64,64]{1,3,2,0:T(8,128)S(1)} fusion(f32[64,64,1,1]{0,1,3,2:T(8,128)S(1)} %copy-done.10, f32[2,96,64,64]{1,3,2,0:T(8,128)S(1)} %bitcast.218), kind=kOutput, calls=%fused_computation.54 | convolution fusion | flops 603979776 | bytes 6307840 | tf_op jit(solution)/shard_map/csba,bk->cska/dot_general | solution.py:26
  90.2 6.6 %fusion.60 = f32[2,96,64,64]{1,3,2,0:T(8,128)S(1)} fusion(f32[2,96,64,64]{1,3,2,0:T(8,128)S(1)} %fusion.37, f32[64,64,1,1]{0,1,3,2:T(8,128)S(1)} %copy-done.10, f32[2,96,64,64]{1,3,2,0:T(8,128)S(1)} %bitcast.215), kind=kOutput, calls=%fused_computation.80 | convolution fusion | flops 604766208 | bytes 9453568 | tf_op jit(solution)/shard_map/csba,bk->cska/dot_general | solution.py:26
  96.9 11.2 %fusion.13 = (f32[2,96,64,64]{1,2,3,0:T(8,128)}, f32[2,96,64,64]{1,2,3,0:T(8,128)S(1)}) fusion(f32[2,96,64,64]{1,3,2,0:T(8,128)S(1)} %fusion.60, f32[64,64]{0,1:T(8,128)S(1)} %copy-done.15, f32[64,64]{0,1:T(8,128)S(1)} %copy-done.9, f32[2,96,64,64]{1,3,2,0:T(8,128)S(1)} %fusion.35, f32[64,64,1,1]{0,1,3,2:T(8,128)S(1)} %copy-done.13, ...), kind=kOutput, calls=%fused_computation.20 | convolution fusion | flops 609484800 | bytes 15777792 | tf_op jit(solution)/shard_map/csba,bk->cska/dot_general | solution.py:26
  108.1 7.0 %fusion.29 = f32[2,96,64,64]{1,3,2,0:T(8,128)} fusion(f32[64,64,1,1]{0,1,3,2:T(8,128)S(1)} %copy-done.13, f32[2,96,64,64]{1,2,3,0:T(8,128)S(1)} %get-tuple-element.5), kind=kOutput, calls=%fused_computation.48 | convolution fusion | flops 603979776 | bytes 6307840 | tf_op jit(solution)/shard_map/cska,aj->csjk/dot_general | solution.py:26
  115.1 7.1 %fusion.27 = f32[2,96,64,64]{1,3,2,0:T(8,128)} fusion(f32[64,64,1,1]{0,1,3,2:T(8,128)S(1)} %copy-done.10, f32[2,96,64,64]{1,2,3,0:T(8,128)S(1)} %get-tuple-element.5), kind=kOutput, calls=%fused_computation.46 | convolution fusion | flops 603979776 | bytes 6307840 | tf_op jit(solution)/shard_map/cska,aj->csjk/dot_general | solution.py:26
  127.5 9.7 %subtract_bitcast_fusion.1 = f32[2,96,64,64]{1,2,3,0:T(8,128)S(1)} fusion(f32[2,96,64,64]{1,3,2,0:T(8,128)} %fusion.29, f32[64,64,1,1]{0,1,3,2:T(8,128)S(1)} %copy-done.10, f32[2,96,64,64]{1,2,3,0:T(8,128)} %get-tuple-element.4), kind=kOutput, calls=%fused_computation.37 | convolution fusion | flops 604766208 | bytes 9453568 | tf_op jit(solution)/shard_map/cska,aj->csjk/dot_general | solution.py:26
  152.1 9.7 %add_bitcast_fusion.1 = f32[2,96,64,64]{1,2,3,0:T(8,128)S(1)} fusion(f32[2,96,64,64]{1,3,2,0:T(8,128)} %fusion.27, f32[64,64,1,1]{0,1,3,2:T(8,128)S(1)} %copy-done.13, f32[2,96,64,64]{1,2,3,0:T(8,128)} %get-tuple-element.4), kind=kOutput, calls=%fused_computation.36 | convolution fusion | flops 604766208 | bytes 9453568 | tf_op jit(solution)/shard_map/cska,aj->csjk/dot_general | solution.py:26
  166.1 11.3 %fusion.12 = (f32[2,96,4096]{1,2,0:T(8,128)}, f32[2,96,4096]{1,2,0:T(8,128)}) fusion(f32[2,96,4096]{1,2,0:T(8,128)} %copy.195, f32[2,96,64,64]{1,3,2,0:T(8,128)} %copy.194, s32[2,96,4096]{1,2,0:T(8,128)} %copy.186, f32[2,96,4096]{1,2,0:T(8,128)} %copy.200, f32[2,96,64,64]{1,3,2,0:T(8,128)} %copy.199), kind=kLoop, calls=%fused_computation.17 | loop fusion | flops 3932160 | bytes 22020096 | tf_op jit(solution)/shard_map/mul | solution.py:83
  177.4 10.9 %fusion.19 = f32[2,96,64,64]{1,3,2,0:T(8,128)} fusion(f32[64,64,1,1]{0,1,3,2:T(8,128)S(1)} %copy-done.10, f32[2,96,64,64]{1,3,2,0:T(8,128)} %bitcast.227), kind=kOutput, calls=%fused_computation.38 | convolution fusion | flops 603979776 | bytes 6307840 | tf_op jit(solution)/shard_map/csjk,ja->cska/dot_general | solution.py:26
  188.3 7.1 %fusion.21 = f32[2,96,64,64]{1,3,2,0:T(8,128)} fusion(f32[64,64,1,1]{0,1,3,2:T(8,128)S(1)} %copy-done.12, f32[2,96,64,64]{1,3,2,0:T(8,128)S(1)} %bitcast.228), kind=kOutput, calls=%fused_computation.40 | convolution fusion | flops 603979776 | bytes 6307840 | tf_op jit(solution)/shard_map/csjk,ja->cska/dot_general | solution.py:26
  195.3 7.1 %fusion.23 = f32[2,96,64,64]{1,3,2,0:T(8,128)} fusion(f32[64,64,1,1]{0,1,3,2:T(8,128)S(1)} %copy-done.12, f32[2,96,64,64]{1,3,2,0:T(8,128)S(1)} %bitcast.225), kind=kOutput, calls=%fused_computation.42 | convolution fusion | flops 603979776 | bytes 6307840 | tf_op jit(solution)/shard_map/csjk,ja->cska/dot_general | solution.py:26
  202.5 7.2 %fusion.25 = f32[2,96,64,64]{1,3,2,0:T(8,128)} fusion(f32[64,64,1,1]{0,1,3,2:T(8,128)S(1)} %copy-done.10, f32[2,96,64,64]{1,3,2,0:T(8,128)S(1)} %bitcast.226), kind=kOutput, calls=%fused_computation.44 | convolution fusion | flops 603979776 | bytes 6307840 | tf_op jit(solution)/shard_map/csjk,ja->cska/dot_general | solution.py:26
  209.7 17.0 %copy_add_fusion = (f32[2,96,64,64]{1,2,3,0:T(8,128)S(1)}, f32[2,96,64,64]{1,2,3,0:T(8,128)}) fusion(f32[2,96,64,64]{1,3,2,0:T(8,128)} %fusion.19, f32[2,96,64,64]{1,3,2,0:T(8,128)} %fusion.23, f32[2,96,64,64]{1,3,2,0:T(8,128)} %fusion.21, f32[2,96,64,64]{1,3,2,0:T(8,128)} %fusion.25), kind=kLoop, calls=%fused_computation.29 | loop fusion | flops 1572864 | bytes 18874368 | tf_op jit(solution)/shard_map/add | solution.py:59
  226.7 6.7 %fusion.74 = f32[2,96,64,64]{1,3,2,0:T(8,128)S(1)} fusion(f32[64,64,1,1]{0,1,3,2:T(8,128)S(1)} %copy-done.12, f32[2,96,64,64]{1,2,3,0:T(8,128)S(1)} %get-tuple-element.26, f32[2,96,64,64]{1,2,3,0:T(8,128)} %get-tuple-element.27, f32[64,64]{0,1:T(8,128)S(1)} %copy-done.11, f32[64,64]{0,1:T(8,128)S(1)} %copy-done.9), kind=kOutput, calls=%fused_computation.85 | convolution fusion | flops 606339072 | bytes 9486336 | tf_op jit(solution)/shard_map/cska,kb->csba/dot_general | solution.py:26
  256.2 7.4 %fusion.70 = f32[2,64,64,96]{3,2,1,0:T(8,128)} fusion(f32[2,64,64,96]{3,2,1,0:T(8,128)S(1)} %fusion.15, f32[96,96,1,1]{1,0,3,2:T(8,128)S(1)} %copy-done.18, f32[2,96,64,64]{1,2,3,0:T(8,128)S(1)} %subtract_bitcast_fusion), kind=kOutput, calls=%fused_computation.82 | convolution fusion | flops 906756096 | bytes 9474048 | tf_op jit(solution)/shard_map/csba,sr->crba/dot_general | solution.py:26
  284.9 7.8 %copy.211 = f32[2,96,32,134]{3,2,1,0:T(8,128)} copy(f32[2,96,32,134]{1,3,2,0:T(8,128)} %pad_maximum_fusion) | data formatting | bytes 6586368 | tf_op jit(solution)/shard_map/concatenate | solution.py:167
  292.7 8.3 %fusion.128 = f32[2,96,32,128]{3,2,1,0:T(8,128)} fusion(f32[2,96,32,134]{3,2,1,0:T(8,128)} %copy.211, f32[134,128,1,1]{1,0,3,2:T(8,128)S(1)} %copy-done.17), kind=kOutput, calls=%fused_computation.170 | convolution fusion | flops 1264582656 | bytes 6507520 | tf_op jit(solution)/shard_map/...m,mk->...k/dot_general | solution.py:26
  325.3 8.4 %fusion.43 = f32[2,96,32,64]{1,3,2,0:T(8,128)S(1)} fusion(f32[70,64,1,1]{0,1,3,2:T(8,128)S(1)} %copy-done.22, f32[2,96,32,70]{3,2,1,0:T(8,128)S(1)} %maximum_maximum_fusion), kind=kOutput, calls=%fused_computation.63 | convolution fusion | flops 330301440 | bytes 3311104 | tf_op jit(solution)/shard_map/...m,mk->...k/dot_general | solution.py:26
  342.0 7.0 %multiply_reduce_fusion = (f32[96,32,128]{0,2,1:T(8,128)}, f32[2,96,32,128]{1,3,2,0:T(8,128)}) fusion(f32[2,96,32,64]{1,3,2,0:T(8,128)} %copy.233, f32[2,96,32,32]{1,3,2,0:T(8,128)} %get-tuple-element.23, f32[2,96,32,16]{1,3,2,0:T(8,128)} %get-tuple-element.25, f32[2,96,32,16]{1,3,2,0:T(8,128)S(1)} %fusion.106, f32[32,2,96,128]{2,3,0,1:T(8,128)} %copy.210), kind=kLoop, calls=%fused_computation.31 | loop fusion | flops 5111808 | bytes 11010048 | tf_op jit(solution)/shard_map/reduce_sum | solution.py:208
  349.0 135.1 %all-reduce.2.cloned.1.call-done = f32[96,4096]{0,1:T(8,128)} async-done(((f32[96,4096]{0,1:T(8,128)}), f32[96,4096]{0,1:T(8,128)}) %all-reduce.2.cloned.1.call-update) | async-done | bytes 1572880 | tf_op jit(solution)/shard_map/psum | solution.py:208
  487.0 15.1 %copy_divide_fusion = f32[2,96,4096]{1,0,2:T(2,128)S(1)} fusion(f32[2,96,4096]{1,2,0:T(8,128)S(1)} %bitcast.232, f32[96,4096]{0,1:T(8,128)S(1)} %multiply_maximum_fusion), kind=kLoop, calls=%fused_computation.24 | loop fusion | flops 786432 | bytes 7864320 | tf_op jit(solution)/shard_map/div | solution.py:209
  502.1 97.1 %all_to_all.23 = f32[2,96,4096]{1,0,2:T(2,128)} all-to-all(f32[2,96,4096]{1,0,2:T(2,128)S(1)} %copy_divide_fusion), channel_id=1, replica_groups=mesh['groups'=1,'fac'=32] {'fac'}, dimensions={2} | all-to-all | bytes 6291456 | tf_op jit(solution)/shard_map/all_to_all | solution.py:210
  599.2 6.6 %copy.217 = f32[32,2,96,128]{3,2,1,0:T(8,128)} copy(f32[32,2,96,128]{2,1,3,0:T(2,128)} %bitcast.234) | data formatting | bytes 6291456 | tf_op jit(solution)/shard_map/all_to_all | solution.py:210
  (143 shorter events, 172.4 us)
Async XLA Ops:
  39.5 24.6 %copy-start.5 = (f32[2,96,4096]{2,1,0:T(8,128)S(1)}, f32[2,96,4096]{2,1,0:T(8,128)}, u32[]{:S(2)}) copy-start(f32[2,96,4096]{2,1,0:T(8,128)} %param.30) | copy-start | bytes 9437188
  56.6 212.3 %all-to-all-start = ((f32[32,2,96,128]{3,2,1,0:T(8,128)}), f32[32,2,96,128]{3,2,1,0:T(8,128)}, u32[]{:S(2)}, u32[]{:S(2)}) async-start(f32[32,2,96,128]{3,2,1,0:T(8,128)} %bitcast_dynamic-update-slice_fusion), calls=%async_computation | async-start | bytes 6291456 | tf_op jit(solution)/shard_map/all_to_all | solution.py:187
  64.0 3.4 copy-start.20
  64.0 420.2 %all-reduce.2.cloned.1.call-start = ((), (), s32[]{:S(2)}) async-start(), calls=%async_computation.2 | async-start | bytes 4194304 | tf_op jit(solution)/shard_map/psum | solution.py:208
  67.4 5.8 copy-start.1
  67.4 5.8 copy-start.21
  73.2 3.6 copy-start.13
  76.8 6.6 %copy-start.10 = (f32[64,64,1,1]{0,1,3,2:T(8,128)S(1)}, f32[64,64,1,1]{0,1,3,2:T(8,128)}, u32[]{:S(2)}) copy-start(f32[64,64,1,1]{0,1,3,2:T(8,128)} %constant.72) | copy-start | bytes 49156
  90.2 6.6 %copy-start.9 = (f32[64,64]{0,1:T(8,128)S(1)}, f32[64,64]{0,1:T(8,128)}, u32[]{:S(2)}) copy-start(f32[64,64]{0,1:T(8,128)} %constant.55.clone) | copy-start | bytes 49156
  90.2 6.6 %copy-start.15 = (f32[64,64]{0,1:T(8,128)S(1)}, f32[64,64]{0,1:T(8,128)}, u32[]{:S(2)}) copy-start(f32[64,64]{0,1:T(8,128)} %constant.56.clone) | copy-start | bytes 49156
  177.4 10.9 %copy-start.4 = (f32[2,96,4096]{1,2,0:T(8,128)S(1)}, f32[2,96,4096]{1,2,0:T(8,128)}, u32[]{:S(2)}) copy-start(f32[2,96,4096]{1,2,0:T(8,128)} %get-tuple-element.19) | copy-start | bytes 9437188
  177.4 10.9 %copy-start.12 = (f32[64,64,1,1]{0,1,3,2:T(8,128)S(1)}, f32[64,64,1,1]{0,1,3,2:T(8,128)}, u32[]{:S(2)}) copy-start(f32[64,64,1,1]{0,1,3,2:T(8,128)} %constant.74) | copy-start | bytes 49156
  188.3 7.1 %copy-start.3 = (f32[2,96,4096]{1,2,0:T(8,128)S(1)}, f32[2,96,4096]{1,2,0:T(8,128)}, u32[]{:S(2)}) copy-start(f32[2,96,4096]{1,2,0:T(8,128)} %get-tuple-element.18) | copy-start | bytes 9437188
  209.7 17.0 %copy-start.11 = (f32[64,64]{0,1:T(8,128)S(1)}, f32[64,64]{0,1:T(8,128)}, u32[]{:S(2)}) copy-start(f32[64,64]{0,1:T(8,128)} %constant.58.clone) | copy-start | bytes 49156
  226.7 6.7 %copy-start = (f32[2,96,64,64]{1,2,3,0:T(8,128)S(1)}, f32[2,96,64,64]{1,2,3,0:T(8,128)}, u32[]{:S(2)}) copy-start(f32[2,96,64,64]{1,2,3,0:T(8,128)} %get-tuple-element.27) | copy-start | bytes 9437188
  233.4 5.6 copy-start.19
  250.8 5.4 copy-start.18
  274.1 3.2 copy-start.27
  284.9 7.8 %copy-start.17 = (f32[134,128,1,1]{1,0,3,2:T(8,128)S(1)}, f32[134,128,1,1]{1,0,3,2:T(8,128)}, u32[]{:S(2)}) copy-start(f32[134,128,1,1]{1,0,3,2:T(8,128)} %constant.80) | copy-start | bytes 205828
  300.9 4.9 copy-start.6
  300.9 5.0 copy-start.14
  312.2 3.4 copy-start.8
  325.3 9.6 %copy-start.23 = (f32[38,32,1,1]{0,1,3,2:T(8,128)S(1)}, f32[38,32,1,1]{0,1,3,2:T(8,128)}, u32[]{:S(2)}) copy-start(f32[38,32,1,1]{0,1,3,2:T(8,128)} %constant.84) | copy-start | bytes 14596
  336.1 4.2 copy-start.24
  (6 other events, 11.5 us)
Sparse Core Ops, SparseCore 0:
  349.1 134.9 all-reduce.1
